TPU v7x, 512 devices: a whole 4x8x8 slice. The times are simulated.
512 devices in a mesh: row: 32 (over z_lo, y), col: 16 (over x, z_hi, core).
Axes of the slice: x: 4, y: 8, z: 8 (z_hi: 2, z_lo: 4; z = z_hi * 4 + z_lo), core: 2. Of those that a mesh axis runs over, the one named last changes fastest.
Arguments:
- eigvecs: float32 [8192, 2048], P('row', 'col'), may hold values from -6 to 6
- reflectors: float32 [8, 32, 256, 512], P(None, 'row', 'col'), may hold values from -1 to 1
- factors: float32 [8, 32, 256, 256], P(None, 'row', 'col'), as said below
- offsets: int32 [8, 32], P(None, 'row'), may hold values from 0 to 255
- sweep_order: int32 [8], replicated, may hold values from 0 to 7, each once
Outputs:
- rotated: float32 [8192, 2048], P('row', 'col')
Inputs may be any that keep to these rules, and one draw needn't show every extreme that they name: `factors`: zero below the diagonal. `sweep_order`: each number of 0 to 7 appears once; only the first 2 entries are used.
All inputs are finite; a program needn't handle non-finite values.
Results may differ from a plain program's by a relative error of at most 0.0003.
Values sent between devices are 32-bit elements; how exact they have to be, the bound alone decides.
A program may use at most 64 MiB of HBM per device.

v0:
```python
import jax
import jax.numpy as jnp
from jax import lax
from jax.sharding import PartitionSpec as P

PRECISE = lax.Precision.HIGHEST


def from_behind(block, axis, distance):
    devices = range(lax.axis_size(axis))
    route = [(i - distance, i) for i in devices if i - distance in devices]
    return lax.ppermute(block, axis, route)


def carried_in(value, axis, join, neutral):
    count, mine = (lax.axis_size(axis), lax.axis_index(axis))
    pieces = jax.tree.map(lambda part: lax.all_gather(part, axis), value)
    running = jax.tree.map(
        lambda part, zero: jnp.full_like(part, 0) + jnp.asarray(zero, part.dtype), value, neutral
    )

    def hop(position, running):
        longer = join(running, jax.tree.map(lambda part: part[position], pieces))
        return jax.tree.map(lambda new, old: jnp.where(position < mine, new, old), longer, running)

    return lax.fori_loop(0, count - 1, hop, running)


def matmul(left_side, right_side):
    return jnp.dot(left_side, right_side, precision=PRECISE, preferred_element_type=jnp.float32)


def transposed_product(left_side, right_side):
    return lax.dot_general(
        left_side,
        right_side,
        (((0,), (0,)), ((), ())),
        precision=PRECISE,
        preferred_element_type=jnp.float32,
    )


def staircase(raw_entries, start_shift, column_base):
    reflector_count, height = raw_entries.shape
    reflector = column_base + lax.broadcasted_iota(jnp.int32, (reflector_count, height), 0)
    position = lax.broadcasted_iota(jnp.int32, (reflector_count, height), 1)
    start_row = reflector + start_shift
    live_mask = (position >= start_row) & (position < start_row + height // 2)
    kept = jnp.where(live_mask, raw_entries, jnp.zeros_like(raw_entries))
    return jnp.where(position == start_row, jnp.ones_like(raw_entries), kept)


def local_set(reflectors, factors, offsets, which, column_base):
    raw_entries = lax.dynamic_index_in_dim(reflectors, which, 0, keepdims=False)[0]
    start_shift = lax.dynamic_index_in_dim(offsets, which, 0, keepdims=False)[0]
    factor = lax.dynamic_index_in_dim(factors, which, 0, keepdims=False)[0]
    return (staircase(raw_entries, start_shift, column_base), factor)


def set_terms(vectors, factor, seed_rows, below_rows):
    half = factor.shape[0]
    upper_part = vectors[:, :half]
    lower_part = vectors[:, half:]
    below_proj = matmul(lower_part, below_rows)
    coeffs = matmul(factor, matmul(upper_part, seed_rows) + below_proj)
    seed_top = seed_rows - transposed_product(upper_part, coeffs)
    seed_low = below_rows - transposed_product(lower_part, coeffs)
    factor_upper = matmul(factor, upper_part)
    return (upper_part, lower_part, below_proj, seed_top, seed_low, factor_upper)


def finish(upper_part, factor, below_proj, carry_in):
    coeffs = matmul(factor, matmul(upper_part, carry_in) + below_proj)
    return carry_in - transposed_product(upper_part, coeffs)


def compose(earlier_map, later_map):
    early_gain, early_shift = earlier_map
    late_gain, late_shift = later_map
    return (matmul(late_gain, early_gain), matmul(late_gain, early_shift) + late_shift)


def on_device(eigvecs, reflectors, factors, offsets, sweep_order):
    height = eigvecs.shape[0]
    leading = lax.axis_index("row") == 0
    column_base = lax.axis_index("col") * reflectors.shape[2]
    lead_local = local_set(reflectors, factors, offsets, sweep_order[0], column_base)
    tail_local = local_set(reflectors, factors, offsets, sweep_order[1], column_base)
    joined_vectors, joined_factors = (
        lax.all_gather(jnp.stack([lead_local[0], tail_local[0]]), "col", axis=1, tiled=True),
        lax.all_gather(jnp.stack([lead_local[1], tail_local[1]]), "col", axis=1, tiled=True),
    )
    lead_set = (joined_vectors[0], joined_factors[0])
    below_rows = from_behind(eigvecs, "row", -1)
    slab_zero = jnp.zeros_like(eigvecs)
    seed_rows = jnp.where(leading, eigvecs, slab_zero)
    upper_part, lower_part, below_proj, seed_top, seed_low, factor_upper = set_terms(
        lead_set[0], lead_set[1], seed_rows, below_rows
    )
    identity = jnp.eye(height, dtype=jnp.float32)
    square_zero = jnp.zeros_like(identity)
    link_map = jnp.where(leading, square_zero, -transposed_product(lower_part, factor_upper))
    prefix = carried_in((link_map, seed_low), "row", compose, (identity, slab_zero))
    carry_in = prefix[1] + seed_rows
    finished = finish(upper_part, lead_set[1], below_proj, carry_in)
    tail_set = (joined_vectors[1], joined_factors[1])
    below_two = from_behind(finished, "row", -1)
    seed_two = jnp.where(leading, finished, slab_zero)
    two_upper, two_lower, two_proj, two_top, two_low, two_factor_upper = set_terms(
        tail_set[0], tail_set[1], seed_two, below_two
    )
    link_two = jnp.where(leading, square_zero, -transposed_product(two_lower, two_factor_upper))
    prefix_two = carried_in((link_two, two_low), "row", compose, (identity, slab_zero))
    carry_two = prefix_two[1] + seed_two
    rotated = finish(two_upper, tail_set[1], two_proj, carry_two)
    return rotated


def solution(mesh):
    placed = (
        P("row", "col"),
        P(None, "row", "col", None),
        P(None, "row", "col", None),
        P(None, "row"),
        P(),
    )
    return jax.shard_map(
        on_device, mesh=mesh, in_specs=placed, out_specs=P("row", "col"), check_vma=False
    )
```

profile of v0, /device:TPU:2, one launch (start us, length us, event | category | flops | bytes accessed | tf_op | source)
XLA Modules:
  0.0 782.1 jit_solution(15657264733518081436)
XLA Ops:
  6.5 1.4 fusion.58
  12.0 1.4 constant_dynamic-slice_fusion.1
  18.3 35.3 %all_gather.31 = f32[2,256,256]{2,1,0:T(8,128)S(1)} all-gather(f32[2,16,256]{2,1,0:T(8,128)S(1)} %pad_maximum_fusion.1), channel_id=1, replica_groups=mesh['row'=32,'col'=16] {'col'}, dimensions={1}, use_global_device_ids=true | all-gather | bytes 557056 | tf_op jit(solution)/shard_map/all_gather | solution.py:91
  53.6 30.6 %all-gather.10.cloned.1.call-done = f32[2,256,512]{2,1,0:T(8,128)} async-done(((f32[2,16,512]{2,1,0:T(8,128)}), f32[2,256,512]{2,1,0:T(8,128)}) %all-gather.10.cloned.1.call-update) | async-done | bytes 1048592 | tf_op jit(solution)/shard_map/all_gather | solution.py:90
  92.4 150.2 %all-gather.16.cloned.1.call-done = f32[8192,128]{1,0:T(8,128)} async-done(((f32[256,128]{1,0:T(8,128)}), f32[8192,128]{1,0:T(8,128)}) %all-gather.16.cloned.1.call-update) | async-done | bytes 4194320 | tf_op jit(solution)/shard_map/all_gather | solution.py:17
  242.7 165.5 %all-gather.14.cloned.1.call-done = f32[8192,256]{1,0:T(8,128)} async-done(((f32[256,256]{1,0:T(8,128)}), f32[8192,256]{1,0:T(8,128)}) %all-gather.14.cloned.1.call-update) | async-done | bytes 8388624 | tf_op jit(solution)/shard_map/all_gather | solution.py:17
  408.2 44.0 %while.28 = (s32[]{:T(128)}, f32[256,128]{1,0:T(8,128)S(1)}, s32[]{:T(128)}, f32[32,256,256]{2,1,0:T(8,128)}, f32[32,256,128]{2,1,0:T(8,128)}, /*index=5*/s32[]{:T(128)}, s32[]{:T(128)}) while((s32[]{:T(128)}, f32[256,128]{1,0:T(8,128)S(1)}, s32[]{:T(128)}, f32[32,256,256]{2,1,0:T(8,128)}, f32[32,256,128]{2,1,0:T(8,128)}, ...), condition=%wide.region_1.2_spmd.clone, body=%wide.region_0.1_spmd.clone.sunk | while | flops 100794368 | bytes 1051231 | solution.py:26
  408.2 1.4 fusion.79
  409.6 1.4 fusion.79
  411.0 1.4 fusion.79
  412.5 1.4 fusion.79
  415.3 1.4 fusion.79
  416.7 1.4 fusion.79
  418.1 1.4 fusion.79
  419.6 1.4 fusion.79
  422.4 1.4 fusion.79
  423.8 1.4 fusion.79
  425.2 1.4 fusion.79
  426.6 1.4 fusion.79
  428.1 1.4 fusion.79
  429.5 1.4 fusion.79
  430.9 1.4 fusion.79
  432.3 1.4 fusion.79
  433.8 1.4 fusion.79
  435.2 1.4 fusion.79
  436.6 1.4 fusion.79
  438.0 1.4 fusion.79
  439.4 1.4 fusion.79
  440.9 1.4 fusion.79
  442.3 1.4 fusion.79
  443.7 1.4 fusion.79
  445.1 1.4 fusion.79
  446.5 1.4 fusion.79
  448.0 1.4 fusion.79
  449.4 1.4 fusion.79
  450.8 1.4 fusion.79
  454.9 7.7 collective-permute-done.1
  465.0 108.9 %all-gather.12.cloned.1.call-done = f32[8192,256]{1,0:T(8,128)} async-done(((f32[256,256]{1,0:T(8,128)}), f32[8192,256]{1,0:T(8,128)}) %all-gather.12.cloned.1.call-update) | async-done | bytes 8388624 | tf_op jit(solution)/shard_map/all_gather | solution.py:17
  573.9 155.8 %all-gather.18.cloned.1.call-done = f32[8192,128]{1,0:T(8,128)} async-done(((f32[256,128]{1,0:T(8,128)}), f32[8192,128]{1,0:T(8,128)}) %all-gather.18.cloned.1.call-update) | async-done | bytes 4194320 | tf_op jit(solution)/shard_map/all_gather | solution.py:17
  729.6 43.9 %while.29 = (s32[]{:T(128)}, f32[256,128]{1,0:T(8,128)S(1)}, s32[]{:T(128)}, f32[32,256,256]{2,1,0:T(8,128)}, f32[32,256,128]{2,1,0:T(8,128)}, /*index=5*/s32[]{:T(128)}, s32[]{:T(128)}) while((s32[]{:T(128)}, f32[256,128]{1,0:T(8,128)S(1)}, s32[]{:T(128)}, f32[32,256,256]{2,1,0:T(8,128)}, f32[32,256,128]{2,1,0:T(8,128)}, ...), condition=%wide.region_3.4_spmd.clone, body=%wide.region_2.3_spmd.clone.sunk | while | flops 100794368 | bytes 1051231 | solution.py:26
  729.7 1.4 fusion.82
  731.1 1.4 fusion.82
  733.9 1.4 fusion.82
  735.3 1.4 fusion.82
  738.2 1.4 fusion.82
  739.6 1.4 fusion.82
  742.4 1.4 fusion.82
  743.8 1.4 fusion.82
  (128 shorter events, 55.1 us)
Async XLA Ops:
  6.5 445.7 %copy-start = (f32[256,128]{1,0:T(8,128)S(1)}, f32[256,128]{1,0:T(8,128)}, u32[]{:S(2)}) copy-start(f32[256,128]{1,0:T(8,128)} %param.9) | copy-start | bytes 393220
  6.5 77.6 %all-gather.10.cloned.1.call-start = ((), (), s32[]{:S(2)}) async-start(), calls=%async_computation | async-start | bytes 1114112 | tf_op jit(solution)/shard_map/all_gather | solution.py:90
  16.2 226.4 %all-gather.16.cloned.1.call-start = ((), (), s32[]{:S(2)}) async-start(), calls=%async_computation.3 | async-start | bytes 4325376 | tf_op jit(solution)/shard_map/all_gather | solution.py:17
  16.3 69.2 %collective-permute-start = (f32[256,128]{1,0:T(8,128)}, f32[256,128]{1,0:T(8,128)S(1)}, u32[]{:S(2)}, u32[]{:S(2)}) collective-permute-start(f32[256,128]{1,0:T(8,128)} %param.9), channel_id=1, source_target_pairs={{16,0},{32,16},{48,32},{64,48},{80,64},{96,80},{112,96},{128,112},... | collective-permute-start | bytes 393224 | tf_op jit(solution)/shard_map/ppermute | solution.py:12
  88.8 319.4 %all-gather.14.cloned.1.call-start = ((), (), s32[]{:S(2)}) async-start(), calls=%async_computation.2 | async-start | bytes 8650752 | tf_op jit(solution)/shard_map/all_gather | solution.py:17
  90.6 483.3 %all-gather.12.cloned.1.call-start = ((), (), s32[]{:S(2)}) async-start(), calls=%async_computation.1 | async-start | bytes 8650752 | tf_op jit(solution)/shard_map/all_gather | solution.py:17
  92.4 637.3 %all-gather.18.cloned.1.call-start = ((), (), s32[]{:S(2)}) async-start(), calls=%async_computation.4 | async-start | bytes 4325376 | tf_op jit(solution)/shard_map/all_gather | solution.py:17
  453.6 9.0 %collective-permute-start.1 = (f32[256,128]{1,0:T(8,128)S(1)}, f32[256,128]{1,0:T(8,128)S(1)}, u32[]{:S(2)}, u32[]{:S(2)}) collective-permute-start(f32[256,128]{1,0:T(8,128)S(1)} %convolution_subtract_fusion.2), channel_id=1, source_target_pairs={{16,0},{32,16},{48,32},{64,48},{80,64},{96,80},{112,96},{128,112},... | collective-permute-start | bytes 393224 | tf_op jit(solution)/shard_map/ppermute | solution.py:12
Sparse Core Ops, SparseCore 0:
  16.4 67.7 all-gather.9
  88.9 153.6 all-gather.15
  244.8 163.3 all-gather.13
  410.1 163.7 all-gather.11
  575.8 153.7 all-gather.17
where the time goes:
time: 784 us; the launch traced here: 782 us
  waiting for transfers between devices  619 us (79%)
  matrix products  97.5 us (12%)
  blocking collectives  35.3 us (5%)
  between operations  17.3 us (2%)
    all_gather x4, waiting for transfers between devices, carried_in(): pieces = jax.tree.map(lambda part: lax.all_gather(part, axis), value)  580 us
    dot_general x74, matrix products, matmul(): jnp.dot(left_side, right_side, precision=PRECISE, preferred_element_type=...  90.4 us
    all_gather x1, blocking collectives, on_device(): lax.all_gather(jnp.stack([lead_local[1], tail_local[1]]), 'col', axis=1,...  35.3 us
    all_gather x1, waiting for transfers between devices, on_device(): lax.all_gather(jnp.stack([lead_local[0], tail_local[0]]), 'col', axis=1,...  30.6 us
  transfers between devices with their start and end apart: 7, of which 6 were waited for; matrix products, arithmetic and copies ran while one was open for 7% of the time, Pallas kernels for 0%

commit v1 on v0

v1 whole, which is shorter than its diff:
```python
import functools

import jax
import jax.numpy as jnp
from jax import lax
from jax.experimental import pallas as pl
from jax.experimental.pallas import tpu as pltpu
from jax.sharding import PartitionSpec as P

MESH = pl.DeviceIdType.MESH
F32, BF16 = jnp.float32, jnp.bfloat16
NN, NT = ((1,), (0,)), ((1,), (1,))

Z_LO, Y, X, Z_HI, CORES = 4, 8, 4, 2, 2


def split(value):
    high = value.astype(BF16)
    return high, (value - high.astype(F32)).astype(BF16)


def dot(left, right, dims):
    return lax.dot_general(left, right, (dims, ((), ())), preferred_element_type=F32)


def product(left, right, dims):
    (lh, ll), (rh, rl) = left, right
    return dot(lh, rh, dims) + (dot(lh, rl, dims) + dot(ll, rh, dims))


def kernel(
    dims,
    order_ref,
    offs_ref,
    eig_ref,
    refl_ref,
    fact_ref,
    out_ref,
    vf,
    ops_h,
    ops_l,
    proj,
    below_raw,
    below,
    init,
    gains,
    gains_h,
    gains_l,
    d_out,
    d_in,
    carry_in,
    carry_out,
    states_out,
    states_in,
    z_s,
    z_r,
    x_s,
    x_r,
    q_s,
    q_r,
    e_s,
    e_r,
    g_s,
    g_r,
    gq_s,
    gq_r,
    d_s,
    d_r,
    i_s,
    c_s,
    c_r,
    s_s,
    s_r,
    f_s,
    f_r,
):
    KZ, NY, NX, NH, NQ = dims
    NB = eig_ref.shape[0]
    CL = eig_ref.shape[1]
    CW = CL // NY
    RC = refl_ref.shape[2]
    HALF = NB // NQ
    PART = HALF // 2
    FAR = NY // 2

    row, col = lax.axis_index("row"), lax.axis_index("col")
    k, y = row // NY, row % NY
    x, h, q = col // (NH * NQ), (col // NQ) % NH, col % NQ
    last_row = KZ * NY - 1

    def y_peer(d):
        return (k * NY + (y + d) % NY, col)

    def x_peer(d):
        return (row, ((x + d) % NX) * (NH * NQ) + h * NQ + q)

    z_peer = (row, x * (NH * NQ) + (1 - h) * NQ + q)
    sibling = (row, x * (NH * NQ) + h * NQ + (1 - q))
    up_group, down_group = (row - NY, col), (row + NY, col)
    up_row, down_row = (row - 1, col), (row + 1, col)

    def copy(src, dst, ssem, rsem, device):
        return pltpu.make_async_remote_copy(
            src_ref=src,
            dst_ref=dst,
            send_sem=ssem,
            recv_sem=rsem,
            device_id=device,
            device_id_type=MESH,
        )

    def arrived(dst, rsem):
        copy(dst, dst, z_s.at[0], rsem, sibling).wait_recv()

    barrier = pltpu.get_barrier_semaphore()

    def greet(device):
        pl.semaphore_signal(barrier, inc=1, device_id=device, device_id_type=MESH)

    greet(z_peer)
    greet(sibling)
    for d in range(1, NX):
        greet(x_peer(d))
    for d in range(1, NY):
        greet(y_peer(d))
    has_up, has_down = k > 0, k < KZ - 1
    first_y, final_y = y == 0, y == NY - 1

    @pl.when(has_up)
    def _():
        greet(up_group)

    @pl.when(has_down)
    def _():
        greet(down_group)

    @pl.when(has_up & first_y)
    def _():
        greet(up_row)

    @pl.when(has_down & final_y)
    def _():
        greet(down_row)

    def start_of(t):
        return offs_ref[order_ref[t], 0]

    for t in range(2):
        chosen = order_ref[t]
        raw = refl_ref[chosen, 0]
        start = (
            col * RC + start_of(t) + lax.broadcasted_iota(jnp.int32, (RC, NB), 0)
        )
        position = lax.broadcasted_iota(jnp.int32, (RC, NB), 1)
        upper, lower = raw[:, :NB], raw[:, NB:]
        packed = jnp.where(position + NB >= start, lower, jnp.zeros_like(lower))
        packed = jnp.where(position >= start, upper, packed)
        unit = (position == start) | (position + NB == start)
        vf[t, x, h, q, pl.ds(0, RC)] = jnp.where(unit, jnp.ones_like(packed), packed)
        vf[t, x, h, q, pl.ds(RC, RC)] = fact_ref[chosen, 0]

    expected = (
        2
        + (NX - 1)
        + (NY - 1)
        + has_up.astype(jnp.int32)
        + has_down.astype(jnp.int32)
        + (has_up & first_y).astype(jnp.int32)
        + (has_down & final_y).astype(jnp.int32)
    )
    pl.semaphore_wait(barrier, expected)

    def z_send(t):
        piece = vf.at[t, x, h, q]
        return copy(piece, piece, z_s.at[t], z_r.at[t], z_peer)

    def x_send(t, p, d):
        piece = vf.at[t, x, h if p == 0 else 1 - h, q]
        return copy(piece, piece, x_s.at[t, p, d], x_r.at[t, p, d], x_peer(d))

    def q_send(t, p, d):
        piece = vf.at[t, (x + NX - d) % NX, h if p == 0 else 1 - h, q]
        return copy(piece, piece, q_s.at[t, p, d], q_r.at[t, p, d], sibling)

    def x_take(t, p, d):
        piece = vf.at[t, (x + NX - d) % NX, h if p == 0 else 1 - h, q]
        arrived(piece, x_r.at[t, p, d])
        q_send(t, p, d).start()

    def q_take(t):
        for p in range(NH):
            for d in range(NX):
                piece = vf.at[t, (x + NX - d) % NX, h if p == 0 else 1 - h, 1 - q]
                arrived(piece, q_r.at[t, p, d])

    def z_take(t):
        arrived(vf.at[t, x, 1 - h, q], z_r.at[t])
        for d in range(1, NX):
            x_send(t, 1, d).start()
        q_send(t, 1, 0).start()

    def e_send():
        return copy(eig_ref, below_raw, e_s, e_r, up_row)

    near_first = sorted(range(1, NX), key=lambda d: min(d, NX - d))
    for t in range(2):
        z_send(t).start()
    for t in range(2):
        for d in near_first:
            x_send(t, 0, d).start()
        q_send(t, 0, 0).start()

    @pl.when(row > 0)
    def _():
        e_send().start()

    def init_send(t, d):
        there = pl.ds(((y + d) % NY) * CW, CW)
        return copy(
            init.at[t, there], carry_in.at[t], i_s.at[t, d], c_r.at[t], y_peer(d)
        )

    def send_init(t):
        for d in range(1, NY):
            init_send(t, d).start()
        carry_in[t] = init[t, pl.ds(0, CW)]

    @pl.when(row == 0)
    def _():
        init[0] = jnp.transpose(eig_ref[...])
        send_init(0)

    z_take(0)
    for d in near_first:
        x_take(0, 0, d)
    z_take(1)
    for d in near_first:
        x_take(0, 1, d)

    @pl.when(row < last_row)
    def _():
        arrived(below_raw, e_r)
        below[0] = jnp.transpose(below_raw[...])

    @pl.when(row == last_row)
    def _():
        below[0] = jnp.zeros((CL, NB), F32)

    q_take(0)

    UP, LOW, FAC = 0, 1, 2

    def parts(t, which):
        return ops_h[t, which], ops_l[t, which]

    def unpack(t):
        both = vf[t, :, :, :, pl.ds(0, RC), :].reshape(NB, NB)
        factor = vf[t, :, :, :, pl.ds(RC, RC), :].reshape(NB, NB)
        start = lax.broadcasted_iota(jnp.int32, (NB, NB), 0) + start_of(t)
        position = lax.broadcasted_iota(jnp.int32, (NB, NB), 1)
        zero = jnp.zeros_like(both)
        for which, value in (
            (UP, jnp.where(position >= start, both, zero)),
            (LOW, jnp.where(position < start, both, zero)),
            (FAC, factor),
        ):
            ops_h[t, which], ops_l[t, which] = split(value)

    def make_gain(t):
        inner = product(parts(t, FAC), parts(t, UP), NN)
        turned = jnp.transpose(inner)
        gains[t, y] = -product(split(turned), parts(t, LOW), NN)

    def make_shift(t):
        rows = below[t]
        lowered = product(split(rows), parts(t, LOW), NT)
        proj[t] = lowered
        coeffs = product(split(lowered), parts(t, FAC), NT)
        d_out[t] = rows - product(split(coeffs), parts(t, LOW), NN)

    def finish(t):
        rows = states_in[t]
        coeffs = product(split(rows), parts(t, UP), NT) + proj[t]
        coeffs = product(split(coeffs), parts(t, FAC), NT)
        return rows - product(split(coeffs), parts(t, UP), NN)

    def ring_ids():
        for d in range(1, FAR + 1):
            for m in range(2):
                for way in range(2):
                    if d < FAR or m == way:
                        yield way, d, m

    def part_rows(m):
        return pl.ds(pl.multiple_of(q * HALF + m * PART, PART), PART)

    def ring_send(t, way, d, m):
        source = (y + NY - (d - 1)) % NY if way == 0 else (y + (d - 1)) % NY
        piece = gains.at[t, source, part_rows(m)]
        there = y_peer(1 if way == 0 else NY - 1)
        return copy(
            piece, piece, g_s.at[t, way, d, m], g_r.at[t, way, d, m], there
        )

    def ring_source(way, d):
        return (y + NY - d) % NY if way == 0 else (y + d) % NY

    def ring_pass(t, way, d, m):
        piece = gains.at[t, ring_source(way, d), part_rows(m)]
        return copy(
            piece, piece, gq_s.at[t, way, d, m], gq_r.at[t, way, d, m], sibling
        )

    def ring_start(t):
        for way, d, m in ring_ids():
            if d == 1:
                ring_send(t, way, d, m).start()

    def ring_run(t):
        ids = list(ring_ids())
        for way, d, m in ids:
            arrived(
                gains.at[t, ring_source(way, d), part_rows(m)], g_r.at[t, way, d, m]
            )
            if (way, d + 1, m) in ids:
                ring_send(t, way, d + 1, m).start()
            ring_pass(t, way, d, m).start()
        for way, d, m in ids:
            other = pl.ds(pl.multiple_of((1 - q) * HALF + m * PART, PART), PART)
            arrived(gains.at[t, ring_source(way, d), other], gq_r.at[t, way, d, m])

        def convert(i, carry):
            gains_h[t, i], gains_l[t, i] = split(gains[t, i])
            return carry

        lax.fori_loop(0, NY, convert, 0)

    def d_send(t, d):
        there = pl.ds(((y + d) % NY) * CW, CW)
        return copy(
            d_out.at[t, there], d_in.at[t, y], d_s.at[t, d], d_r.at[t, d], y_peer(d)
        )

    def send_shift(t):
        for d in range(1, NY):
            d_send(t, d).start()
        d_in[t, y] = d_out[t, pl.ds(y * CW, CW)]

    def take_shift(t):
        for d in range(1, NY):
            arrived(d_in.at[t, (y + NY - d) % NY], d_r.at[t, d])

    def state_send(t, i):
        return copy(
            states_out.at[t, i],
            states_in.at[t, pl.ds(y * CW, CW)],
            s_s.at[t, i],
            s_r.at[t, y],
            (k * NY + i, col),
        )

    def carry_send(t):
        return copy(carry_out.at[t], carry_in.at[t], c_s.at[t], c_r.at[t], down_group)

    def chain(t):
        take_shift(t)

        @pl.when(row > 0)
        def _():
            arrived(carry_in.at[t], c_r.at[t])

        state = carry_in[t]
        for i in range(NY):
            states_out[t, i] = state

            @pl.when(y != i)
            def _():
                state_send(t, i).start()

            high, low = split(state)
            gain_h = gains_h[t, i]
            pair = dot(jnp.concatenate([high, low], 0), gain_h, NN)
            state = (pair[:CW] + pair[CW:]) + (
                dot(high, gains_l[t, i], NN) + d_in[t, i]
            )
        carry_out[t] = state

        @pl.when(has_down)
        def _():
            carry_send(t).start()

    def collect(t):
        mine = pl.ds(y * CW, CW)
        states_in[t, mine] = states_out[t, y]
        for d in range(1, NY):
            source = (y + d) % NY
            arrived(states_in.at[t, pl.ds(source * CW, CW)], s_r.at[t, source])

    def f_send():
        return copy(init.at[1], below.at[1], f_s, f_r, up_row)

    unpack(0)
    make_gain(0)
    ring_start(0)
    make_shift(0)
    send_shift(0)
    for d in near_first:
        x_take(1, 0, d)
    for d in near_first:
        x_take(1, 1, d)
    q_take(1)
    unpack(1)
    make_gain(1)
    ring_run(0)

    @pl.when(k >= KZ // 2)
    def _():
        ring_start(1)
        ring_run(1)

    chain(0)

    @pl.when(k < KZ // 2)
    def _():
        ring_start(1)
        ring_run(1)

    collect(0)
    init[1] = finish(0)

    @pl.when(row > 0)
    def _():
        f_send().start()

    @pl.when(row == 0)
    def _():
        send_init(1)

    @pl.when(row < last_row)
    def _():
        arrived(below.at[1], f_r)

    @pl.when(row == last_row)
    def _():
        below[1] = jnp.zeros((CL, NB), F32)

    make_shift(1)
    send_shift(1)
    chain(1)
    collect(1)
    out_ref[...] = jnp.transpose(finish(1))

    for t in range(2):
        z_send(t).wait_send()
        for p in range(NH):
            for d in range(NX):
                if d:
                    x_send(t, p, d).wait_send()
                q_send(t, p, d).wait_send()
        for way, d, m in ring_ids():
            ring_send(t, way, d, m).wait_send()
            ring_pass(t, way, d, m).wait_send()
        for d in range(1, NY):
            d_send(t, d).wait_send()
        for i in range(NY):

            @pl.when(y != i)
            def _():
                state_send(t, i).wait_send()

        @pl.when(has_down)
        def _():
            carry_send(t).wait_send()

        @pl.when(row == 0)
        def _():
            for d in range(1, NY):
                init_send(t, d).wait_send()

    @pl.when(row > 0)
    def _():
        e_send().wait_send()
        f_send().wait_send()


def on_device(dims, eigvecs, reflectors, factors, offsets, sweep_order):
    KZ, NY, NX, NH, NQ = dims
    NB, CL = eigvecs.shape
    CW = CL // NY
    RC = reflectors.shape[2]
    FAR = NY // 2
    DMA = pltpu.SemaphoreType.DMA
    vmem = pl.BlockSpec(memory_space=pltpu.VMEM)
    smem = pl.BlockSpec(memory_space=pltpu.SMEM)
    return pl.pallas_call(
        functools.partial(kernel, dims),
        out_shape=jax.ShapeDtypeStruct((NB, CL), F32),
        in_specs=[smem, smem, vmem, vmem, vmem],
        out_specs=vmem,
        scratch_shapes=[
            pltpu.VMEM((2, NX, NH, NQ, 2 * RC, NB), F32),
            pltpu.VMEM((2, 3, NB, NB), BF16),
            pltpu.VMEM((2, 3, NB, NB), BF16),
            pltpu.VMEM((2, CL, NB), F32),
            pltpu.VMEM((NB, CL), F32),
            pltpu.VMEM((2, CL, NB), F32),
            pltpu.VMEM((2, CL, NB), F32),
            pltpu.VMEM((2, NY, NB, NB), F32),
            pltpu.VMEM((2, NY, NB, NB), BF16),
            pltpu.VMEM((2, NY, NB, NB), BF16),
            pltpu.VMEM((2, CL, NB), F32),
            pltpu.VMEM((2, NY, CW, NB), F32),
            pltpu.VMEM((2, CW, NB), F32),
            pltpu.VMEM((2, CW, NB), F32),
            pltpu.VMEM((2, NY, CW, NB), F32),
            pltpu.VMEM((2, CL, NB), F32),
            DMA((2,)),
            DMA((2,)),
            DMA((2, NH, NX)),
            DMA((2, NH, NX)),
            DMA((2, NH, NX)),
            DMA((2, NH, NX)),
            DMA,
            DMA,
            DMA((2, 2, FAR + 1, 2)),
            DMA((2, 2, FAR + 1, 2)),
            DMA((2, 2, FAR + 1, 2)),
            DMA((2, 2, FAR + 1, 2)),
            DMA((2, NY)),
            DMA((2, NY)),
            DMA((2, NY)),
            DMA((2,)),
            DMA((2,)),
            DMA((2, NY)),
            DMA((2, NY)),
            DMA,
            DMA,
        ],
        compiler_params=pltpu.CompilerParams(collective_id=0, has_side_effects=True),
    )(sweep_order, offsets, eigvecs, reflectors, factors)


def build(mesh, dims):
    placed = (
        P("row", "col"),
        P(None, "row", "col", None),
        P(None, "row", "col", None),
        P(None, "row"),
        P(),
    )
    return jax.shard_map(
        functools.partial(on_device, dims),
        mesh=mesh,
        in_specs=placed,
        out_specs=P("row", "col"),
        check_vma=False,
    )


def solution(mesh):
    return build(mesh, (Z_LO, Y, X, Z_HI, CORES))
```

time: 784 us -> 101 us (0.13)
  the two profiles are of different devices: /device:TPU:2 before, /device:TPU:248 now
where the time goes in v1:
time: 101 us
  Pallas kernels  97.7 us (97%)
  local copies, waits for them, and re-layouts  2.89 us (3%)
    pallas_call x1, Pallas kernels, on_device(): pl.pallas_call(functools.partial(kernel, dims), out_shape=jax.ShapeDtypeS...  97.7 us
    unnamed x2, local copies, waits for them, and re-layouts  2.89 us

profile of v1, /device:TPU:248, one launch (start us, length us, event | category | flops | bytes accessed | tf_op | source)
XLA Modules:
  0.0 100.6 jit_solution(9060310774738404991)
XLA Ops:
  0.0 1.3 %copy.6.offs_ref = s32[8,1]{1,0:T(8,128)} copy(s32[8,1]{0,1:T(1,128)} %param.8) | data formatting | bytes 64 | tf_op args[3]
  1.3 97.7 %shard_map.55 = f32[256,128]{1,0:T(8,128)} custom-call(s32[8]{0:T(128)} %order_ref.1, s32[8,1]{1,0:T(8,128)} %copy.6.offs_ref, f32[256,128]{1,0:T(8,128)} %eig_ref.1, f32[8,1,16,512]{3,2,1,0:T(8,128)} %refl_ref.1, f32[8,1,16,256]{3,2,1,0:T(8,128)} %fact_ref.1), custom_call_target="tpu_custom_call" | custom-call | tf_op jit(solution)/shard_map/pallas_call | solution.py:495
  99.0 1.6 %copy.8 = f32[256,128]{1,0:T(8,128)} copy(f32[256,128]{1,0:T(8,128)} %shard_map.55) | data formatting | bytes 262144

commit v2 on v1

--- a/solution.py
+++ b/solution.py
@@ -49,9 +49,12 @@
     d_out,
     d_in,
     carry_in,
-    carry_out,
     states_out,
     states_in,
+    back_out,
+    back_in,
+    rest_out,
+    rest_in,
     z_s,
     z_r,
     x_s,
@@ -71,17 +74,25 @@
     c_r,
     s_s,
     s_r,
-    f_s,
-    f_r,
+    a_s,
+    a_r,
+    h_s,
+    h_r,
+    ax_s,
+    ax_r,
+    aq_s,
+    aq_r,
 ):
     KZ, NY, NX, NH, NQ = dims
     NB = eig_ref.shape[0]
     CL = eig_ref.shape[1]
     CW = CL // NY
     RC = refl_ref.shape[2]
-    HALF = NB // NQ
-    PART = HALF // 2
+    HB = NB // 2
+    SHARE = HB // NQ
+    PART = SHARE // 2
     FAR = NY // 2
+    BACK = NB // (NX * NQ)
 
     row, col = lax.axis_index("row"), lax.axis_index("col")
     k, y = row // NY, row % NY
@@ -143,7 +154,7 @@
         greet(down_row)
 
     def start_of(t):
-        return offs_ref[order_ref[t], 0]
+        return offs_ref[order_ref[t]]
 
     for t in range(2):
         chosen = order_ref[t]
@@ -176,11 +187,11 @@
 
     def x_send(t, p, d):
         piece = vf.at[t, x, h if p == 0 else 1 - h, q]
-        return copy(piece, piece, x_s.at[t, p, d], x_r.at[t, p, d], x_peer(d))
+        return copy(piece, piece, x_s.at[t], x_r.at[t, p, d], x_peer(d))
 
     def q_send(t, p, d):
         piece = vf.at[t, (x + NX - d) % NX, h if p == 0 else 1 - h, q]
-        return copy(piece, piece, q_s.at[t, p, d], q_r.at[t, p, d], sibling)
+        return copy(piece, piece, q_s.at[t], q_r.at[t], sibling)
 
     def x_take(t, p, d):
         piece = vf.at[t, (x + NX - d) % NX, h if p == 0 else 1 - h, q]
@@ -188,10 +199,7 @@
         q_send(t, p, d).start()
 
     def q_take(t):
-        for p in range(NH):
-            for d in range(NX):
-                piece = vf.at[t, (x + NX - d) % NX, h if p == 0 else 1 - h, 1 - q]
-                arrived(piece, q_r.at[t, p, d])
+        arrived(vf.at[t, :, :, 0], q_r.at[t])
 
     def z_take(t):
         arrived(vf.at[t, x, 1 - h, q], z_r.at[t])
@@ -202,6 +210,7 @@
     def e_send():
         return copy(eig_ref, below_raw, e_s, e_r, up_row)
 
+    y_far_first = sorted(range(1, NY), key=lambda d: -min(d, NY - d))
     near_first = sorted(range(1, NX), key=lambda d: min(d, NX - d))
     for t in range(2):
         z_send(t).start()
@@ -217,7 +226,7 @@
     def init_send(t, d):
         there = pl.ds(((y + d) % NY) * CW, CW)
         return copy(
-            init.at[t, there], carry_in.at[t], i_s.at[t, d], c_r.at[t], y_peer(d)
+            init.at[t, there], carry_in.at[t], i_s.at[t], c_r.at[t], y_peer(d)
         )
 
     def send_init(t):
@@ -268,18 +277,45 @@
 
     def make_gain(t):
         inner = product(parts(t, FAC), parts(t, UP), NN)
-        turned = jnp.transpose(inner)
-        gains[t, y] = -product(split(turned), parts(t, LOW), NN)
+        turned = split(jnp.transpose(inner))
+        gain = -product(turned, parts(t, LOW), NN)
+        gains[t, y, :, :HB] = gain[:HB, :HB] + jnp.transpose(gain[HB:, HB:])
+        gains[t, y, :, HB:] = gain[HB:, :HB]
+        return turned
+
+    def spread_gain(t, i):
+        square, corner = gains[t, i, :, :HB], gains[t, i, :, HB:]
+        down = lax.broadcasted_iota(jnp.int32, (HB, HB), 0)
+        across = lax.broadcasted_iota(jnp.int32, (HB, HB), 1)
+        zero = jnp.zeros_like(square)
+        first = jnp.where(down > across, square, zero)
+        second = jnp.transpose(jnp.where(across > down, square, zero))
+        for r, c, value in (
+            (0, 0, first),
+            (0, 1, zero),
+            (1, 0, corner),
+            (1, 1, second),
+        ):
+            high, low = split(value)
+            gains_h[t, i, r * HB : (r + 1) * HB, c * HB : (c + 1) * HB] = high
+            gains_l[t, i, r * HB : (r + 1) * HB, c * HB : (c + 1) * HB] = low
 
     def make_shift(t):
         rows = below[t]
         lowered = product(split(rows), parts(t, LOW), NT)
         proj[t] = lowered
-        coeffs = product(split(lowered), parts(t, FAC), NT)
-        d_out[t] = rows - product(split(coeffs), parts(t, LOW), NN)
-
-    def finish(t):
-        rows = states_in[t]
+        coeffs = split(product(split(lowered), parts(t, FAC), NT))
+        d_out[t] = rows - product(coeffs, parts(t, LOW), NN)
+        return coeffs
+
+    def make_back(turned, coeffs):
+        down = lax.broadcasted_iota(jnp.int32, (NB, NB), 0)
+        across = lax.broadcasted_iota(jnp.int32, (NB, NB), 1)
+        unit = jnp.where(down == across, 1.0, 0.0).astype(F32)
+        back_out[...] = unit - product(turned, parts(0, UP), NN)
+        rest_out[...] = -product(coeffs, parts(0, UP), NN)
+
+    def finish(t, rows):
         coeffs = product(split(rows), parts(t, UP), NT) + proj[t]
         coeffs = product(split(coeffs), parts(t, FAC), NT)
         return rows - product(split(coeffs), parts(t, UP), NN)
@@ -291,24 +327,24 @@
                     if d < FAR or m == way:
                         yield way, d, m
 
-    def part_rows(m):
-        return pl.ds(pl.multiple_of(q * HALF + m * PART, PART), PART)
+    def part_rows(m, core):
+        return pl.ds(pl.multiple_of(core * SHARE + m * PART, PART), PART)
 
     def ring_send(t, way, d, m):
         source = (y + NY - (d - 1)) % NY if way == 0 else (y + (d - 1)) % NY
-        piece = gains.at[t, source, part_rows(m)]
+        piece = gains.at[t, source, part_rows(m, q)]
         there = y_peer(1 if way == 0 else NY - 1)
         return copy(
-            piece, piece, g_s.at[t, way, d, m], g_r.at[t, way, d, m], there
+            piece, piece, g_s.at[t], g_r.at[t, way, d - 1, m], there
         )
 
     def ring_source(way, d):
         return (y + NY - d) % NY if way == 0 else (y + d) % NY
 
     def ring_pass(t, way, d, m):
-        piece = gains.at[t, ring_source(way, d), part_rows(m)]
+        piece = gains.at[t, ring_source(way, d), part_rows(m, q)]
         return copy(
-            piece, piece, gq_s.at[t, way, d, m], gq_r.at[t, way, d, m], sibling
+            piece, piece, gq_s.at[t], gq_r.at[t, d - 1], sibling
         )
 
     def ring_start(t):
@@ -316,51 +352,61 @@
             if d == 1:
                 ring_send(t, way, d, m).start()
 
-    def ring_run(t):
+    def ring_step(t, distance):
         ids = list(ring_ids())
         for way, d, m in ids:
+            if d != distance:
+                continue
             arrived(
-                gains.at[t, ring_source(way, d), part_rows(m)], g_r.at[t, way, d, m]
+                gains.at[t, ring_source(way, d), part_rows(m, q)], g_r.at[t, way, d - 1, m]
             )
             if (way, d + 1, m) in ids:
                 ring_send(t, way, d + 1, m).start()
             ring_pass(t, way, d, m).start()
-        for way, d, m in ids:
-            other = pl.ds(pl.multiple_of((1 - q) * HALF + m * PART, PART), PART)
-            arrived(gains.at[t, ring_source(way, d), other], gq_r.at[t, way, d, m])
-
-        def convert(i, carry):
-            gains_h[t, i], gains_l[t, i] = split(gains[t, i])
-            return carry
-
-        lax.fori_loop(0, NY, convert, 0)
+
+    def ring_land(t, distance):
+        pieces = 2 if distance == FAR else 4
+        arrived(gains.at[t, 0, pl.ds(0, pieces * PART)], gq_r.at[t, distance - 1])
+        for way in range(1 if distance == FAR else 2):
+            spread_gain(t, ring_source(way, distance))
 
     def d_send(t, d):
         there = pl.ds(((y + d) % NY) * CW, CW)
         return copy(
-            d_out.at[t, there], d_in.at[t, y], d_s.at[t, d], d_r.at[t, d], y_peer(d)
+            d_out.at[t, there], d_in.at[t, y], d_s.at[t], d_r.at[t], y_peer(d)
         )
 
     def send_shift(t):
-        for d in range(1, NY):
+        for d in y_far_first:
             d_send(t, d).start()
         d_in[t, y] = d_out[t, pl.ds(y * CW, CW)]
 
     def take_shift(t):
-        for d in range(1, NY):
-            arrived(d_in.at[t, (y + NY - d) % NY], d_r.at[t, d])
+        arrived(d_in.at[t, pl.ds(0, NY - 1)], d_r.at[t])
+
+    def owner_of(t, i):
+        return i - 1 if t == 0 else i
 
     def state_send(t, i):
         return copy(
             states_out.at[t, i],
             states_in.at[t, pl.ds(y * CW, CW)],
-            s_s.at[t, i],
-            s_r.at[t, y],
-            (k * NY + i, col),
-        )
+            s_s.at[t],
+            s_r.at[t],
+            (k * NY + owner_of(t, i), col),
+        )
+
+    def share_state(t, i):
+        if 0 <= owner_of(t, i) < NY:
+
+            @pl.when(y != owner_of(t, i))
+            def _():
+                state_send(t, i).start()
 
     def carry_send(t):
-        return copy(carry_out.at[t], carry_in.at[t], c_s.at[t], c_r.at[t], down_group)
+        return copy(
+            states_out.at[t, NY], carry_in.at[t], c_s.at[t], c_r.at[t], down_group
+        )
 
     def chain(t):
         take_shift(t)
@@ -372,73 +418,184 @@
         state = carry_in[t]
         for i in range(NY):
             states_out[t, i] = state
-
-            @pl.when(y != i)
-            def _():
-                state_send(t, i).start()
-
+            share_state(t, i)
             high, low = split(state)
             gain_h = gains_h[t, i]
             pair = dot(jnp.concatenate([high, low], 0), gain_h, NN)
             state = (pair[:CW] + pair[CW:]) + (
                 dot(high, gains_l[t, i], NN) + d_in[t, i]
             )
-        carry_out[t] = state
+        states_out[t, NY] = state
 
         @pl.when(has_down)
         def _():
             carry_send(t).start()
+
+        share_state(t, NY)
 
     def collect(t):
         mine = pl.ds(y * CW, CW)
-        states_in[t, mine] = states_out[t, y]
-        for d in range(1, NY):
-            source = (y + d) % NY
-            arrived(states_in.at[t, pl.ds(source * CW, CW)], s_r.at[t, source])
-
-    def f_send():
-        return copy(init.at[1], below.at[1], f_s, f_r, up_row)
+        states_in[t, mine] = states_out[t, y + (1 - t)]
+        arrived(states_in.at[t, pl.ds(0, (NY - 1) * CW)], s_r.at[t])
+
+    def back_rows(column, core):
+        at = (column * NQ + core) * BACK
+        return pl.ds(pl.multiple_of(at, BACK), BACK)
+
+    def a_send():
+        rows = back_rows(x, q)
+        return copy(back_out.at[rows], back_in.at[rows], a_s, a_r, up_row)
+
+    def h_send():
+        return copy(rest_out, rest_in, h_s, h_r, up_row)
+
+    def ax_send(d):
+        piece = back_in.at[back_rows(x, q)]
+        return copy(piece, piece, ax_s, ax_r.at[d - 1], x_peer(d))
+
+    def aq_send(d):
+        piece = back_in.at[back_rows((x + NX - d) % NX, q)]
+        return copy(piece, piece, aq_s, aq_r, sibling)
+
+    def back_take():
+        @pl.when(row < last_row)
+        def _():
+            arrived(back_in.at[back_rows(x, q)], a_r)
+            for d in near_first:
+                ax_send(d).start()
+            aq_send(0).start()
+
+    def back_pass():
+        @pl.when(row < last_row)
+        def _():
+            for d in near_first:
+                arrived(back_in.at[back_rows((x + NX - d) % NX, q)], ax_r.at[d - 1])
+                aq_send(d).start()
+
+    def back_land():
+        arrived(back_in.at[pl.ds(0, NX * BACK)], aq_r)
+        arrived(rest_in, h_r)
+
+    def left(view, sem):
+        copy(view, view, sem, z_r.at[0], sibling).wait_send()
+
+    def left_early():
+        for t in range(2):
+            z_send(t).wait_send()
+            left(vf.at[t, pl.ds(0, NX - 1), :, 0], x_s.at[t])
+            left(vf.at[t, :, :, 0], q_s.at[t])
+
+        @pl.when(row > 0)
+        def _():
+            e_send().wait_send()
+
+    def left_ring(t):
+        sent = gains.at[t, pl.ds(0, NY - 1), pl.ds(0, HB // 2)]
+        left(sent, g_s.at[t])
+        left(sent, gq_s.at[t])
+        left(d_out.at[t, pl.ds(0, (NY - 1) * CW)], d_s.at[t])
+
+    def left_back():
+        @pl.when(row > 0)
+        def _():
+            a_send().wait_send()
+            h_send().wait_send()
+
+        @pl.when(row < last_row)
+        def _():
+            left(back_in.at[pl.ds(0, (NX - 1) * BACK)], ax_s)
+            left(back_in.at[pl.ds(0, NX * BACK)], aq_s)
+
+        @pl.when(row == 0)
+        def _():
+            for t in range(2):
+                left(init.at[t, pl.ds(0, (NY - 1) * CW)], i_s.at[t])
+
+    def left_states(t):
+        left(states_out.at[t, pl.ds(0, NY - 1)], s_s.at[t])
+
+        @pl.when(has_down)
+        def _():
+            carry_send(t).wait_send()
 
     unpack(0)
-    make_gain(0)
+    turned = make_gain(0)
     ring_start(0)
-    make_shift(0)
+    coeffs = make_shift(0)
     send_shift(0)
-    for d in near_first:
-        x_take(1, 0, d)
-    for d in near_first:
-        x_take(1, 1, d)
-    q_take(1)
-    unpack(1)
-    make_gain(1)
-    ring_run(0)
-
-    @pl.when(k >= KZ // 2)
-    def _():
+    spread_gain(0, y)
+    make_back(turned, coeffs)
+
+    def ring_slot(t, d):
+        if d <= FAR:
+            ring_step(t, d)
+            if d > 1:
+                ring_land(t, d - 1)
+            if d == FAR:
+                ring_land(t, d)
+
+    for d in range(1, FAR + 1):
+        ring_slot(0, d)
+
+    @pl.when(row > 0)
+    def _():
+        a_send().start()
+        h_send().start()
+
+    def second_set():
+        for p in range(2):
+            for d in near_first:
+                x_take(1, p, d)
+        q_take(1)
+        unpack(1)
+        make_gain(1)
         ring_start(1)
-        ring_run(1)
+        spread_gain(1, y)
+
+    @pl.when(k >= 1)
+    def _():
+        second_set()
+
+    @pl.when(k >= 2)
+    def _():
+        back_take()
+        ring_slot(1, 1)
+        back_pass()
+
+    @pl.when(k >= 3)
+    def _():
+        ring_slot(1, 2)
 
     chain(0)
 
-    @pl.when(k < KZ // 2)
-    def _():
-        ring_start(1)
-        ring_run(1)
-
+    @pl.when(k < 1)
+    def _():
+        second_set()
+
+    @pl.when(k < 2)
+    def _():
+        back_take()
+        ring_slot(1, 1)
+        back_pass()
+
+    @pl.when(k == 2)
+    def _():
+        ring_slot(1, 2)
+
+    @pl.when(k >= 3)
+    def _():
+        ring_slot(1, 3)
+
+    left_early()
+    left_ring(0)
     collect(0)
-    init[1] = finish(0)
-
-    @pl.when(row > 0)
-    def _():
-        f_send().start()
-
-    @pl.when(row == 0)
-    def _():
-        send_init(1)
 
     @pl.when(row < last_row)
     def _():
-        arrived(below.at[1], f_r)
+        back_land()
+        below[1] = rest_in[...] + product(
+            split(states_in[0]), split(back_in[...]), NN
+        )
 
     @pl.when(row == last_row)
     def _():
@@ -446,41 +603,29 @@
 
     make_shift(1)
     send_shift(1)
+
+    @pl.when(row == 0)
+    def _():
+        init[1] = finish(0, init[0])
+        send_init(1)
+
+    @pl.when(k < 2)
+    def _():
+        ring_slot(1, 2)
+
+    @pl.when(k < 3)
+    def _():
+        ring_slot(1, 3)
+
+    for d in range(4, FAR + 1):
+        ring_slot(1, d)
     chain(1)
+    left_ring(1)
+    left_states(0)
+    left_back()
     collect(1)
-    out_ref[...] = jnp.transpose(finish(1))
-
-    for t in range(2):
-        z_send(t).wait_send()
-        for p in range(NH):
-            for d in range(NX):
-                if d:
-                    x_send(t, p, d).wait_send()
-                q_send(t, p, d).wait_send()
-        for way, d, m in ring_ids():
-            ring_send(t, way, d, m).wait_send()
-            ring_pass(t, way, d, m).wait_send()
-        for d in range(1, NY):
-            d_send(t, d).wait_send()
-        for i in range(NY):
-
-            @pl.when(y != i)
-            def _():
-                state_send(t, i).wait_send()
-
-        @pl.when(has_down)
-        def _():
-            carry_send(t).wait_send()
-
-        @pl.when(row == 0)
-        def _():
-            for d in range(1, NY):
-                init_send(t, d).wait_send()
-
-    @pl.when(row > 0)
-    def _():
-        e_send().wait_send()
-        f_send().wait_send()
+    out_ref[...] = jnp.transpose(finish(1, states_in[1]))
+    left_states(1)
 
 
 def on_device(dims, eigvecs, reflectors, factors, offsets, sweep_order):
@@ -505,39 +650,48 @@
             pltpu.VMEM((NB, CL), F32),
             pltpu.VMEM((2, CL, NB), F32),
             pltpu.VMEM((2, CL, NB), F32),
-            pltpu.VMEM((2, NY, NB, NB), F32),
+            pltpu.VMEM((2, NY, NB // 2, NB), F32),
             pltpu.VMEM((2, NY, NB, NB), BF16),
             pltpu.VMEM((2, NY, NB, NB), BF16),
             pltpu.VMEM((2, CL, NB), F32),
             pltpu.VMEM((2, NY, CW, NB), F32),
             pltpu.VMEM((2, CW, NB), F32),
-            pltpu.VMEM((2, CW, NB), F32),
-            pltpu.VMEM((2, NY, CW, NB), F32),
+            pltpu.VMEM((2, NY + 1, CW, NB), F32),
             pltpu.VMEM((2, CL, NB), F32),
+            pltpu.VMEM((NB, NB), F32),
+            pltpu.VMEM((NB, NB), F32),
+            pltpu.VMEM((CL, NB), F32),
+            pltpu.VMEM((CL, NB), F32),
+            DMA((2,)),
             DMA((2,)),
             DMA((2,)),
             DMA((2, NH, NX)),
-            DMA((2, NH, NX)),
-            DMA((2, NH, NX)),
-            DMA((2, NH, NX)),
-            DMA,
-            DMA,
-            DMA((2, 2, FAR + 1, 2)),
-            DMA((2, 2, FAR + 1, 2)),
-            DMA((2, 2, FAR + 1, 2)),
-            DMA((2, 2, FAR + 1, 2)),
-            DMA((2, NY)),
-            DMA((2, NY)),
-            DMA((2, NY)),
-            DMA((2,)),
-            DMA((2,)),
-            DMA((2, NY)),
-            DMA((2, NY)),
+            DMA((2,)),
+            DMA((2,)),
+            DMA,
+            DMA,
+            DMA((2,)),
+            DMA((2, 2, FAR, 2)),
+            DMA((2,)),
+            DMA((2, FAR)),
+            DMA((2,)),
+            DMA((2,)),
+            DMA((2,)),
+            DMA((2,)),
+            DMA((2,)),
+            DMA((2,)),
+            DMA((2,)),
+            DMA,
+            DMA,
+            DMA,
+            DMA,
+            DMA,
+            DMA((NX - 1,)),
             DMA,
             DMA,
         ],
         compiler_params=pltpu.CompilerParams(collective_id=0, has_side_effects=True),
-    )(sweep_order, offsets, eigvecs, reflectors, factors)
+    )(sweep_order, offsets.reshape(-1), eigvecs, reflectors, factors)
 
 
 def build(mesh, dims):

time: 101 us -> 79.8 us (0.79)
  the two profiles are of different devices: /device:TPU:248 before, /device:TPU:208 now
where the time goes in v2:
time: 79.8 us; the launch traced here: 79.7 us
  Pallas kernels  78.1 us (98%)
  local copies, waits for them, and re-layouts  1.57 us (2%)
    pallas_call x1, Pallas kernels, on_device(): pl.pallas_call(functools.partial(kernel, dims), out_shape=jax.ShapeDtypeS...  78.1 us

profile of v2, /device:TPU:208, one launch (start us, length us, event | category | flops | bytes accessed | tf_op | source)
XLA Modules:
  0.0 79.7 jit_solution(13099630288649468007)
XLA Ops:
  0.0 78.1 %shard_map.55 = f32[256,128]{1,0:T(8,128)} custom-call(s32[8]{0:T(128)} %order_ref.1, s32[8]{0:T(128)} %bitcast.1, f32[256,128]{1,0:T(8,128)} %eig_ref.1, f32[8,1,16,512]{3,2,1,0:T(8,128)} %refl_ref.1, f32[8,1,16,256]{3,2,1,0:T(8,128)} %fact_ref.1), custom_call_target="tpu_custom_call" | custom-call | tf_op jit(solution)/shard_map/pallas_call | solution.py:640
  78.1 1.6 %copy.7 = f32[256,128]{1,0:T(8,128)} copy(f32[256,128]{1,0:T(8,128)} %shard_map.55) | data formatting | bytes 262144

commit v3 on v2

--- a/solution.py
+++ b/solution.py
@@ -30,12 +30,19 @@
 
 def kernel(
     dims,
+    order_hbm,
+    offs_hbm,
+    eig_hbm,
+    refl_hbm,
+    fact_hbm,
+    out_hbm,
     order_ref,
     offs_ref,
     eig_ref,
     refl_ref,
     fact_ref,
     out_ref,
+    own_s,
     vf,
     ops_h,
     ops_l,
@@ -123,6 +130,16 @@
     def arrived(dst, rsem):
         copy(dst, dst, z_s.at[0], rsem, sibling).wait_recv()
 
+    loads = [
+        pltpu.make_async_copy(order_hbm, order_ref, own_s.at[4]),
+        pltpu.make_async_copy(offs_hbm, offs_ref, own_s.at[5]),
+        pltpu.make_async_copy(refl_hbm, refl_ref, own_s.at[0]),
+        pltpu.make_async_copy(fact_hbm, fact_ref, own_s.at[1]),
+        pltpu.make_async_copy(eig_hbm, eig_ref, own_s.at[2]),
+    ]
+    for load in loads:
+        load.start()
+
     barrier = pltpu.get_barrier_semaphore()
 
     def greet(device):
@@ -152,6 +169,9 @@
     @pl.when(has_down & final_y)
     def _():
         greet(down_row)
+
+    for load in loads[:4]:
+        load.wait()
 
     def start_of(t):
         return offs_ref[order_ref[t]]
@@ -218,6 +238,8 @@
         for d in near_first:
             x_send(t, 0, d).start()
         q_send(t, 0, 0).start()
+
+    loads[4].wait()
 
     @pl.when(row > 0)
     def _():
@@ -534,57 +556,70 @@
             if d == FAR:
                 ring_land(t, d)
 
-    for d in range(1, FAR + 1):
-        ring_slot(0, d)
-
-    @pl.when(row > 0)
-    def _():
-        a_send().start()
-        h_send().start()
-
-    def second_set():
-        for p in range(2):
-            for d in near_first:
-                x_take(1, p, d)
+    def second_vectors():
         q_take(1)
         unpack(1)
+
+    def second_gain():
         make_gain(1)
-        ring_start(1)
         spread_gain(1, y)
 
+    @pl.when(row > 0)
+    def _():
+        a_send().start()
+
+    ring_step(0, 1)
+    for p in range(2):
+        for d in near_first:
+            x_take(1, p, d)
+    second_vectors()
+    ring_step(0, 2)
+    ring_land(0, 1)
+    back_take()
+    second_gain()
+    for d in range(3, FAR + 1):
+        ring_slot(0, d)
+    if FAR == 2:
+        ring_land(0, FAR)
+    ring_start(1)
+    back_pass()
+
+    def rest_send():
+        @pl.when(row > 0)
+        def _():
+            h_send().start()
+
     @pl.when(k >= 1)
     def _():
-        second_set()
+        rest_send()
 
     @pl.when(k >= 2)
     def _():
-        back_take()
         ring_slot(1, 1)
-        back_pass()
+        ring_slot(1, 2)
 
     @pl.when(k >= 3)
     def _():
+        ring_slot(1, 3)
+
+    chain(0)
+
+    @pl.when(k < 1)
+    def _():
+        rest_send()
+
+    @pl.when(k < 2)
+    def _():
+        ring_slot(1, 1)
         ring_slot(1, 2)
 
-    chain(0)
-
-    @pl.when(k < 1)
-    def _():
-        second_set()
-
-    @pl.when(k < 2)
-    def _():
-        back_take()
-        ring_slot(1, 1)
-        back_pass()
-
     @pl.when(k == 2)
     def _():
-        ring_slot(1, 2)
+        ring_slot(1, 3)
 
     @pl.when(k >= 3)
     def _():
-        ring_slot(1, 3)
+        ring_slot(1, 4)
 
     left_early()
     left_ring(0)
@@ -611,13 +646,13 @@
 
     @pl.when(k < 2)
     def _():
-        ring_slot(1, 2)
+        ring_slot(1, 3)
 
     @pl.when(k < 3)
     def _():
-        ring_slot(1, 3)
-
-    for d in range(4, FAR + 1):
+        ring_slot(1, 4)
+
+    for d in range(5, FAR + 1):
         ring_slot(1, d)
     chain(1)
     left_ring(1)
@@ -625,7 +660,10 @@
     left_back()
     collect(1)
     out_ref[...] = jnp.transpose(finish(1, states_in[1]))
+    store = pltpu.make_async_copy(out_ref, out_hbm, own_s.at[3])
+    store.start()
     left_states(1)
+    store.wait()
 
 
 def on_device(dims, eigvecs, reflectors, factors, offsets, sweep_order):
@@ -635,14 +673,20 @@
     RC = reflectors.shape[2]
     FAR = NY // 2
     DMA = pltpu.SemaphoreType.DMA
-    vmem = pl.BlockSpec(memory_space=pltpu.VMEM)
-    smem = pl.BlockSpec(memory_space=pltpu.SMEM)
+    hbm = pl.BlockSpec(memory_space=pltpu.HBM)
     return pl.pallas_call(
         functools.partial(kernel, dims),
         out_shape=jax.ShapeDtypeStruct((NB, CL), F32),
-        in_specs=[smem, smem, vmem, vmem, vmem],
-        out_specs=vmem,
+        in_specs=[hbm] * 5,
+        out_specs=pl.BlockSpec(memory_space=pl.ANY),
         scratch_shapes=[
+            pltpu.SMEM(sweep_order.shape, jnp.int32),
+            pltpu.SMEM((offsets.shape[0],), jnp.int32),
+            pltpu.VMEM(eigvecs.shape, F32),
+            pltpu.VMEM(reflectors.shape, F32),
+            pltpu.VMEM(factors.shape, F32),
+            pltpu.VMEM(eigvecs.shape, F32),
+            DMA((6,)),
             pltpu.VMEM((2, NX, NH, NQ, 2 * RC, NB), F32),
             pltpu.VMEM((2, 3, NB, NB), BF16),
             pltpu.VMEM((2, 3, NB, NB), BF16),
@@ -690,8 +734,21 @@
             DMA,
             DMA,
         ],
-        compiler_params=pltpu.CompilerParams(collective_id=0, has_side_effects=True),
-    )(sweep_order, offsets.reshape(-1), eigvecs, reflectors, factors)
+        compiler_params=pltpu.CompilerParams(
+            collective_id=0, has_side_effects=True, vmem_limit_bytes=24 << 20
+        ),
+    )(
+        *(
+            pltpu.with_memory_space_constraint(part, pltpu.HBM)
+            for part in (
+                sweep_order,
+                offsets.reshape(-1),
+                eigvecs,
+                reflectors,
+                factors,
+            )
+        ),
+    )
 
 
 def build(mesh, dims):

time: 79.8 us -> 75.8 us (0.950)
  the two profiles are of different devices: /device:TPU:208 before, /device:TPU:192 now
where the time goes in v3:
time: 75.8 us; the launch traced here: 75.6 us
  Pallas kernels  75 us (99%)
    pallas_call x1, Pallas kernels, on_device(): pl.pallas_call(functools.partial(kernel, dims), out_shape=jax.ShapeDtypeS...  75 us

profile of v3, /device:TPU:192, one launch (start us, length us, event | category | flops | bytes accessed | tf_op | source)
XLA Modules:
  0.0 75.6 jit_solution(12920859915941876603)
XLA Ops:
  0.0 75.0 %shard_map.55 = f32[256,128]{1,0:T(8,128)S(1)} custom-call(s32[8]{0:T(128)} %order_hbm.1, s32[8]{0:T(128)} %bitcast.1, f32[256,128]{1,0:T(8,128)} %eig_hbm.1, f32[8,1,16,512]{3,2,1,0:T(8,128)} %refl_hbm.1, f32[8,1,16,256]{3,2,1,0:T(8,128)} %fact_hbm.1), custom_call_target="tpu_custom_call" | custom-call | tf_op jit(solution)/shard_map/pallas_call | solution.py:677
  75.0 0.7 copy.7

commit v4 on v3

--- a/solution.py
+++ b/solution.py
@@ -72,6 +72,8 @@
     e_r,
     g_s,
     g_r,
+    gx_s,
+    gx_r,
     gq_s,
     gq_r,
     d_s,
@@ -97,8 +99,7 @@
     RC = refl_ref.shape[2]
     HB = NB // 2
     SHARE = HB // NQ
-    PART = SHARE // 2
-    FAR = NY // 2
+    PART = SHARE // NX
     BACK = NB // (NX * NQ)
 
     row, col = lax.axis_index("row"), lax.axis_index("col")
@@ -230,14 +231,16 @@
     def e_send():
         return copy(eig_ref, below_raw, e_s, e_r, up_row)
 
+    y_near_first = sorted(range(1, NY), key=lambda d: min(d, NY - d))
     y_far_first = sorted(range(1, NY), key=lambda d: -min(d, NY - d))
     near_first = sorted(range(1, NX), key=lambda d: min(d, NX - d))
-    for t in range(2):
+    def send_own(t):
         z_send(t).start()
-    for t in range(2):
         for d in near_first:
             x_send(t, 0, d).start()
         q_send(t, 0, 0).start()
+
+    send_own(0)
 
     loads[4].wait()
 
@@ -262,9 +265,9 @@
         send_init(0)
 
     z_take(0)
+    send_own(1)
     for d in near_first:
         x_take(0, 0, d)
-    z_take(1)
     for d in near_first:
         x_take(0, 1, d)
 
@@ -342,55 +345,64 @@
         coeffs = product(split(coeffs), parts(t, FAC), NT)
         return rows - product(split(coeffs), parts(t, UP), NN)
 
-    def ring_ids():
-        for d in range(1, FAR + 1):
-            for m in range(2):
-                for way in range(2):
-                    if d < FAR or m == way:
-                        yield way, d, m
-
-    def part_rows(m, core):
-        return pl.ds(pl.multiple_of(core * SHARE + m * PART, PART), PART)
-
-    def ring_send(t, way, d, m):
-        source = (y + NY - (d - 1)) % NY if way == 0 else (y + (d - 1)) % NY
-        piece = gains.at[t, source, part_rows(m, q)]
-        there = y_peer(1 if way == 0 else NY - 1)
-        return copy(
-            piece, piece, g_s.at[t], g_r.at[t, way, d - 1, m], there
-        )
-
-    def ring_source(way, d):
-        return (y + NY - d) % NY if way == 0 else (y + d) % NY
-
-    def ring_pass(t, way, d, m):
-        piece = gains.at[t, ring_source(way, d), part_rows(m, q)]
-        return copy(
-            piece, piece, gq_s.at[t], gq_r.at[t, d - 1], sibling
-        )
-
-    def ring_start(t):
-        for way, d, m in ring_ids():
-            if d == 1:
-                ring_send(t, way, d, m).start()
-
-    def ring_step(t, distance):
-        ids = list(ring_ids())
-        for way, d, m in ids:
-            if d != distance:
-                continue
-            arrived(
-                gains.at[t, ring_source(way, d), part_rows(m, q)], g_r.at[t, way, d - 1, m]
-            )
-            if (way, d + 1, m) in ids:
-                ring_send(t, way, d + 1, m).start()
-            ring_pass(t, way, d, m).start()
-
-    def ring_land(t, distance):
-        pieces = 2 if distance == FAR else 4
-        arrived(gains.at[t, 0, pl.ds(0, pieces * PART)], gq_r.at[t, distance - 1])
-        for way in range(1 if distance == FAR else 2):
-            spread_gain(t, ring_source(way, distance))
+    def share(column, core):
+        at = core * SHARE + column * PART
+        return pl.ds(pl.multiple_of(at, PART), PART)
+
+    def half(core):
+        return pl.ds(pl.multiple_of(core * SHARE, SHARE), SHARE)
+
+    def source_of(d):
+        return (y + NY - d) % NY
+
+    def g_send(t, d):
+        piece = gains.at[t, y, share(x, q)]
+        return copy(piece, piece, g_s.at[t], g_r.at[t, d - 1], y_peer(d))
+
+    def gx_send(t, d, way):
+        piece = gains.at[t, source_of(d), share(x, q)]
+        there = x_peer(1 if way == 0 else NX - 1)
+        return copy(piece, piece, gx_s.at[t], gx_r.at[t, d - 1, way], there)
+
+    def gx_from(way):
+        return (x + NX - 1) % NX if way == 0 else (x + 1) % NX
+
+    def gx_relay(t, d):
+        way = d % 2
+        piece = gains.at[t, source_of(d), share(gx_from(way), q)]
+        there = x_peer(1 if way == 0 else NX - 1)
+        return copy(piece, piece, gx_s.at[t], gx_r.at[t, d - 1, 2], there)
+
+    def gq_send(t, d):
+        piece = gains.at[t, source_of(d), half(q)]
+        return copy(piece, piece, gq_s.at[t], gq_r.at[t, d - 1], sibling)
+
+    def gain_start(t):
+        for d in y_near_first:
+            g_send(t, d).start()
+
+    def gain_take(t, d):
+        arrived(gains.at[t, source_of(d), share(x, q)], g_r.at[t, d - 1])
+        for way in range(2):
+            gx_send(t, d, way).start()
+
+    def gain_relay(t, d):
+        way = d % 2
+        piece = gains.at[t, source_of(d), share(gx_from(way), q)]
+        arrived(piece, gx_r.at[t, d - 1, way])
+        gx_relay(t, d).start()
+
+    def gain_pass(t, d):
+        way = 1 - d % 2
+        piece = gains.at[t, source_of(d), share(gx_from(way), q)]
+        arrived(piece, gx_r.at[t, d - 1, way])
+        far_piece = gains.at[t, source_of(d), share((x + 2) % NX, q)]
+        arrived(far_piece, gx_r.at[t, d - 1, 2])
+        gq_send(t, d).start()
+
+    def gain_land(t, d):
+        arrived(gains.at[t, source_of(d), half(1 - q)], gq_r.at[t, d - 1])
+        spread_gain(t, source_of(d))
 
     def d_send(t, d):
         there = pl.ds(((y + d) % NY) * CW, CW)
@@ -512,9 +524,9 @@
             e_send().wait_send()
 
     def left_ring(t):
-        sent = gains.at[t, pl.ds(0, NY - 1), pl.ds(0, HB // 2)]
-        left(sent, g_s.at[t])
-        left(sent, gq_s.at[t])
+        left(gains.at[t, pl.ds(0, NY - 1), pl.ds(0, PART)], g_s.at[t])
+        left(gains.at[t, pl.ds(0, NY - 1), pl.ds(0, (NX - 1) * PART)], gx_s.at[t])
+        left(gains.at[t, pl.ds(0, NY - 1), pl.ds(0, SHARE)], gq_s.at[t])
         left(d_out.at[t, pl.ds(0, (NY - 1) * CW)], d_s.at[t])
 
     def left_back():
@@ -540,86 +552,88 @@
         def _():
             carry_send(t).wait_send()
 
+    def each(step, t, ds):
+        for d in ds:
+            step(t, d)
+
+    near, far = y_near_first[: NY // 2], y_near_first[NY // 2 :]
     unpack(0)
     turned = make_gain(0)
-    ring_start(0)
+    gain_start(0)
     coeffs = make_shift(0)
+    spread_gain(0, y)
+    z_take(1)
+    each(gain_take, 0, near)
     send_shift(0)
-    spread_gain(0, y)
     make_back(turned, coeffs)
 
-    def ring_slot(t, d):
-        if d <= FAR:
-            ring_step(t, d)
-            if d > 1:
-                ring_land(t, d - 1)
-            if d == FAR:
-                ring_land(t, d)
-
-    def second_vectors():
-        q_take(1)
-        unpack(1)
-
-    def second_gain():
-        make_gain(1)
-        spread_gain(1, y)
-
     @pl.when(row > 0)
     def _():
         a_send().start()
-
-    ring_step(0, 1)
+        h_send().start()
+
+    each(gain_take, 0, far)
+    each(gain_relay, 0, near)
     for p in range(2):
         for d in near_first:
             x_take(1, p, d)
-    second_vectors()
-    ring_step(0, 2)
-    ring_land(0, 1)
+    each(gain_relay, 0, far)
+    each(gain_pass, 0, near)
     back_take()
-    second_gain()
-    for d in range(3, FAR + 1):
-        ring_slot(0, d)
-    if FAR == 2:
-        ring_land(0, FAR)
-    ring_start(1)
-    back_pass()
-
-    def rest_send():
-        @pl.when(row > 0)
-        def _():
-            h_send().start()
+    q_take(1)
+    unpack(1)
+    make_gain(1)
+    gain_start(1)
+    spread_gain(1, y)
+    for d, e in zip(far, near):
+        gain_pass(0, d)
+        gain_land(0, e)
+    for d in y_near_first[len(far) :]:
+        gain_land(0, d)
+
+    def bring():
+        each(gain_take, 1, y_near_first)
+        each(gain_relay, 1, near)
+
+    def relay():
+        each(gain_relay, 1, far)
+
+    def hand():
+        each(gain_pass, 1, y_near_first)
+
+    def keep():
+        each(gain_land, 1, y_near_first)
 
     @pl.when(k >= 1)
     def _():
-        rest_send()
+        back_pass()
 
     @pl.when(k >= 2)
     def _():
-        ring_slot(1, 1)
-        ring_slot(1, 2)
+        bring()
+        relay()
 
     @pl.when(k >= 3)
     def _():
-        ring_slot(1, 3)
+        hand()
 
     chain(0)
 
     @pl.when(k < 1)
     def _():
-        rest_send()
+        back_pass()
 
     @pl.when(k < 2)
     def _():
-        ring_slot(1, 1)
-        ring_slot(1, 2)
+        bring()
 
     @pl.when(k == 2)
     def _():
-        ring_slot(1, 3)
+        hand()
 
     @pl.when(k >= 3)
     def _():
-        ring_slot(1, 4)
+        keep()
 
     left_early()
     left_ring(0)
@@ -646,14 +660,13 @@
 
     @pl.when(k < 2)
     def _():
-        ring_slot(1, 3)
+        relay()
+        hand()
 
     @pl.when(k < 3)
     def _():
-        ring_slot(1, 4)
-
-    for d in range(5, FAR + 1):
-        ring_slot(1, d)
+        keep()
+
     chain(1)
     left_ring(1)
     left_states(0)
@@ -671,7 +684,6 @@
     NB, CL = eigvecs.shape
     CW = CL // NY
     RC = reflectors.shape[2]
-    FAR = NY // 2
     DMA = pltpu.SemaphoreType.DMA
     hbm = pl.BlockSpec(memory_space=pltpu.HBM)
     return pl.pallas_call(
@@ -715,9 +727,11 @@
             DMA,
             DMA,
             DMA((2,)),
-            DMA((2, 2, FAR, 2)),
-            DMA((2,)),
-            DMA((2, FAR)),
+            DMA((2, NY - 1)),
+            DMA((2,)),
+            DMA((2, NY - 1, 3)),
+            DMA((2,)),
+            DMA((2, NY - 1)),
             DMA((2,)),
             DMA((2,)),
             DMA((2,)),

time: 75.8 us -> 69.6 us (0.918)
  Pallas kernels: 75 us -> 68.8 us
    pallas_call x1, Pallas kernels: 75 us -> 68.8 us  [on_device(): pl.pallas_call(functools.partial(kernel, dims), out_shape=jax.ShapeDtypeS...]
where the time goes in v4:
time: 69.6 us; the launch traced here: 69.5 us
  Pallas kernels  68.8 us (99%)
    pallas_call x1, Pallas kernels, on_device(): pl.pallas_call(functools.partial(kernel, dims), out_shape=jax.ShapeDtypeS...  68.8 us

profile of v4, /device:TPU:192, one launch (start us, length us, event | category | flops | bytes accessed | tf_op | source)
XLA Modules:
  0.0 69.5 jit_solution(256198531301241854)
XLA Ops:
  0.0 68.8 %shard_map.55 = f32[256,128]{1,0:T(8,128)S(1)} custom-call(s32[8]{0:T(128)} %order_hbm.1, s32[8]{0:T(128)} %bitcast.1, f32[256,128]{1,0:T(8,128)} %eig_hbm.1, f32[8,1,16,512]{3,2,1,0:T(8,128)} %refl_hbm.1, f32[8,1,16,256]{3,2,1,0:T(8,128)} %fact_hbm.1), custom_call_target="tpu_custom_call" | custom-call | tf_op jit(solution)/shard_map/pallas_call | solution.py:689
  68.8 0.7 copy.7

commit v5 on v4

--- a/solution.py
+++ b/solution.py
@@ -58,6 +58,9 @@
     carry_in,
     states_out,
     states_in,
+    whole_h,
+    whole_l,
+    fresh,
     back_out,
     back_in,
     rest_out,
@@ -442,10 +445,47 @@
             states_out.at[t, NY], carry_in.at[t], c_s.at[t], c_r.at[t], down_group
         )
 
+    middle = has_up & has_down
+
+    def step(t, i, state):
+        high, low = split(state)
+        pair = dot(jnp.concatenate([high, low], 0), gains_h[t, i], NN)
+        return (pair[:CW] + pair[CW:]) + (dot(high, gains_l[t, i], NN) + d_in[t, i])
+
+    def compose(t, with_fresh):
+        whole_h[t], whole_l[t] = gains_h[t, 0], gains_l[t, 0]
+
+        def join(i, state):
+            longer = product(
+                (whole_h[t], whole_l[t]), (gains_h[t, i], gains_l[t, i]), NN
+            )
+            if with_fresh:
+                state = step(t, i, state)
+            whole_h[t], whole_l[t] = split(longer)
+            return state
+
+        state = lax.fori_loop(1, NY, join, d_in[t, 0])
+        if with_fresh:
+            fresh[t] = state
+
     def chain(t):
-        take_shift(t)
-
-        @pl.when(row > 0)
+        if t == 1:
+            take_shift(t)
+
+        @pl.when(middle)
+        def _():
+            if t == 1:
+                state = d_in[t, 0]
+                for i in range(1, NY):
+                    state = step(t, i, state)
+                fresh[t] = state
+            arrived(carry_in.at[t], c_r.at[t])
+            whole = whole_h[t], whole_l[t]
+            states_out[t, NY] = product(split(carry_in[t]), whole, NN) + fresh[t]
+            carry_send(t).start()
+            share_state(t, NY)
+
+        @pl.when((row > 0) & jnp.logical_not(middle))
         def _():
             arrived(carry_in.at[t], c_r.at[t])
 
@@ -453,19 +493,17 @@
         for i in range(NY):
             states_out[t, i] = state
             share_state(t, i)
-            high, low = split(state)
-            gain_h = gains_h[t, i]
-            pair = dot(jnp.concatenate([high, low], 0), gain_h, NN)
-            state = (pair[:CW] + pair[CW:]) + (
-                dot(high, gains_l[t, i], NN) + d_in[t, i]
-            )
-        states_out[t, NY] = state
-
-        @pl.when(has_down)
-        def _():
-            carry_send(t).start()
-
-        share_state(t, NY)
+            state = step(t, i, state)
+
+        @pl.when(jnp.logical_not(middle))
+        def _():
+            states_out[t, NY] = state
+
+            @pl.when(has_down)
+            def _():
+                carry_send(t).start()
+
+            share_state(t, NY)
 
     def collect(t):
         mine = pl.ds(y * CW, CW)
@@ -593,10 +631,9 @@
 
     def bring():
         each(gain_take, 1, y_near_first)
-        each(gain_relay, 1, near)
 
     def relay():
-        each(gain_relay, 1, far)
+        each(gain_relay, 1, y_near_first)
 
     def hand():
         each(gain_pass, 1, y_near_first)
@@ -608,32 +645,40 @@
     def _():
         back_pass()
 
+    @pl.when(middle)
+    def _():
+        take_shift(0)
+        compose(0, True)
+
     @pl.when(k >= 2)
     def _():
         bring()
+
+    @pl.when(k >= 3)
+    def _():
         relay()
 
+    @pl.when(jnp.logical_not(middle))
+    def _():
+        take_shift(0)
+
+    chain(0)
+
+    @pl.when(k < 1)
+    def _():
+        back_pass()
+
+    @pl.when(k < 2)
+    def _():
+        bring()
+
+    @pl.when((k == 1) | (k == 2))
+    def _():
+        relay()
+
     @pl.when(k >= 3)
     def _():
         hand()
-
-    chain(0)
-
-    @pl.when(k < 1)
-    def _():
-        back_pass()
-
-    @pl.when(k < 2)
-    def _():
-        bring()
-
-    @pl.when(k == 2)
-    def _():
-        hand()
-
-    @pl.when(k >= 3)
-    def _():
-        keep()
 
     left_early()
     left_ring(0)
@@ -658,14 +703,19 @@
         init[1] = finish(0, init[0])
         send_init(1)
 
-    @pl.when(k < 2)
+    @pl.when(k < 1)
     def _():
         relay()
+
+    @pl.when(k < 3)
+    def _():
         hand()
 
-    @pl.when(k < 3)
-    def _():
-        keep()
+    keep()
+
+    @pl.when(middle)
+    def _():
+        compose(1, False)
 
     chain(1)
     left_ring(1)
@@ -714,6 +764,9 @@
             pltpu.VMEM((2, CW, NB), F32),
             pltpu.VMEM((2, NY + 1, CW, NB), F32),
             pltpu.VMEM((2, CL, NB), F32),
+            pltpu.VMEM((2, NB, NB), BF16),
+            pltpu.VMEM((2, NB, NB), BF16),
+            pltpu.VMEM((2, CW, NB), F32),
             pltpu.VMEM((NB, NB), F32),
             pltpu.VMEM((NB, NB), F32),
             pltpu.VMEM((CL, NB), F32),

time: 69.6 us -> 67.1 us (0.964)
  Pallas kernels: 68.8 us -> 66.3 us
    pallas_call x1, Pallas kernels: 68.8 us -> 66.3 us  [on_device(): pl.pallas_call(functools.partial(kernel, dims), out_shape=jax.ShapeDtypeS...]
where the time goes in v5:
time: 67.1 us; the launch traced here: 67 us
  Pallas kernels  66.3 us (99%)
    pallas_call x1, Pallas kernels, on_device(): pl.pallas_call(functools.partial(kernel, dims), out_shape=jax.ShapeDtypeS...  66.3 us

profile of v5, /device:TPU:192, one launch (start us, length us, event | category | flops | bytes accessed | tf_op | source)
XLA Modules:
  0.0 67.0 jit_solution(13003192264659595025)
XLA Ops:
  0.0 66.3 %shard_map.55 = f32[256,128]{1,0:T(8,128)S(1)} custom-call(s32[8]{0:T(128)} %order_hbm.1, s32[8]{0:T(128)} %bitcast.1, f32[256,128]{1,0:T(8,128)} %eig_hbm.1, f32[8,1,16,512]{3,2,1,0:T(8,128)} %refl_hbm.1, f32[8,1,16,256]{3,2,1,0:T(8,128)} %fact_hbm.1), custom_call_target="tpu_custom_call" | custom-call | tf_op jit(solution)/shard_map/pallas_call | solution.py:739
  66.3 0.7 copy.7

commit v6 on v5

--- a/solution.py
+++ b/solution.py
@@ -362,19 +362,9 @@
         piece = gains.at[t, y, share(x, q)]
         return copy(piece, piece, g_s.at[t], g_r.at[t, d - 1], y_peer(d))
 
-    def gx_send(t, d, way):
+    def gx_send(t, d, e):
         piece = gains.at[t, source_of(d), share(x, q)]
-        there = x_peer(1 if way == 0 else NX - 1)
-        return copy(piece, piece, gx_s.at[t], gx_r.at[t, d - 1, way], there)
-
-    def gx_from(way):
-        return (x + NX - 1) % NX if way == 0 else (x + 1) % NX
-
-    def gx_relay(t, d):
-        way = d % 2
-        piece = gains.at[t, source_of(d), share(gx_from(way), q)]
-        there = x_peer(1 if way == 0 else NX - 1)
-        return copy(piece, piece, gx_s.at[t], gx_r.at[t, d - 1, 2], there)
+        return copy(piece, piece, gx_s.at[t], gx_r.at[t, d - 1], x_peer(e))
 
     def gq_send(t, d):
         piece = gains.at[t, source_of(d), half(q)]
@@ -386,21 +376,11 @@
 
     def gain_take(t, d):
         arrived(gains.at[t, source_of(d), share(x, q)], g_r.at[t, d - 1])
-        for way in range(2):
-            gx_send(t, d, way).start()
-
-    def gain_relay(t, d):
-        way = d % 2
-        piece = gains.at[t, source_of(d), share(gx_from(way), q)]
-        arrived(piece, gx_r.at[t, d - 1, way])
-        gx_relay(t, d).start()
+        for e in near_first:
+            gx_send(t, d, e).start()
 
     def gain_pass(t, d):
-        way = 1 - d % 2
-        piece = gains.at[t, source_of(d), share(gx_from(way), q)]
-        arrived(piece, gx_r.at[t, d - 1, way])
-        far_piece = gains.at[t, source_of(d), share((x + 2) % NX, q)]
-        arrived(far_piece, gx_r.at[t, d - 1, 2])
+        arrived(gains.at[t, 0, pl.ds(0, (NX - 1) * PART)], gx_r.at[t, d - 1])
         gq_send(t, d).start()
 
     def gain_land(t, d):
@@ -611,18 +591,16 @@
         h_send().start()
 
     each(gain_take, 0, far)
-    each(gain_relay, 0, near)
     for p in range(2):
         for d in near_first:
             x_take(1, p, d)
-    each(gain_relay, 0, far)
-    each(gain_pass, 0, near)
-    back_take()
     q_take(1)
     unpack(1)
     make_gain(1)
     gain_start(1)
     spread_gain(1, y)
+    each(gain_pass, 0, near)
+    back_take()
     for d, e in zip(far, near):
         gain_pass(0, d)
         gain_land(0, e)
@@ -632,9 +610,6 @@
     def bring():
         each(gain_take, 1, y_near_first)
 
-    def relay():
-        each(gain_relay, 1, y_near_first)
-
     def hand():
         each(gain_pass, 1, y_near_first)
 
@@ -654,10 +629,6 @@
     def _():
         bring()
 
-    @pl.when(k >= 3)
-    def _():
-        relay()
-
     @pl.when(jnp.logical_not(middle))
     def _():
         take_shift(0)
@@ -672,11 +643,7 @@
     def _():
         bring()
 
-    @pl.when((k == 1) | (k == 2))
-    def _():
-        relay()
-
-    @pl.when(k >= 3)
+    @pl.when(k >= 2)
     def _():
         hand()
 
@@ -703,11 +670,7 @@
         init[1] = finish(0, init[0])
         send_init(1)
 
-    @pl.when(k < 1)
-    def _():
-        relay()
-
-    @pl.when(k < 3)
+    @pl.when(k < 2)
     def _():
         hand()
 
@@ -782,7 +745,7 @@
             DMA((2,)),
             DMA((2, NY - 1)),
             DMA((2,)),
-            DMA((2, NY - 1, 3)),
+            DMA((2, NY - 1)),
             DMA((2,)),
             DMA((2, NY - 1)),
             DMA((2,)),

time: 67.1 us -> 63.4 us (0.945)
  the two profiles are of different devices: /device:TPU:192 before, /device:TPU:240 now
where the time goes in v6:
time: 63.4 us; the launch traced here: 63.3 us
  Pallas kernels  62.6 us (99%)
  local copies, waits for them, and re-layouts  0.66 us (1%)
    pallas_call x1, Pallas kernels, on_device(): pl.pallas_call(functools.partial(kernel, dims), out_shape=jax.ShapeDtypeS...  62.6 us

profile of v6, /device:TPU:240, one launch (start us, length us, event | category | flops | bytes accessed | tf_op | source)
XLA Modules:
  0.0 63.3 jit_solution(1225693797561844783)
XLA Ops:
  0.0 62.6 %shard_map.55 = f32[256,128]{1,0:T(8,128)S(1)} custom-call(s32[8]{0:T(128)} %order_hbm.1, s32[8]{0:T(128)} %bitcast.1, f32[256,128]{1,0:T(8,128)} %eig_hbm.1, f32[8,1,16,512]{3,2,1,0:T(8,128)} %refl_hbm.1, f32[8,1,16,256]{3,2,1,0:T(8,128)} %fact_hbm.1), custom_call_target="tpu_custom_call" | custom-call | tf_op jit(solution)/shard_map/pallas_call | solution.py:702
  62.7 0.7 %copy.7 = f32[256,128]{1,0:T(8,128)} copy(f32[256,128]{1,0:T(8,128)S(1)} %shard_map.55) | data formatting | bytes 262144

commit v7 on v6

--- a/solution.py
+++ b/solution.py
@@ -600,12 +600,12 @@
     gain_start(1)
     spread_gain(1, y)
     each(gain_pass, 0, near)
-    back_take()
     for d, e in zip(far, near):
         gain_pass(0, d)
         gain_land(0, e)
     for d in y_near_first[len(far) :]:
         gain_land(0, d)
+    back_take()
 
     def bring():
         each(gain_take, 1, y_near_first)
@@ -616,7 +616,7 @@
     def keep():
         each(gain_land, 1, y_near_first)
 
-    @pl.when(k >= 1)
+    @pl.when(k >= 3)
     def _():
         back_pass()
 
@@ -635,13 +635,13 @@
 
     chain(0)
 
-    @pl.when(k < 1)
+    @pl.when(k < 2)
+    def _():
+        bring()
+
+    @pl.when(k < 3)
     def _():
         back_pass()
-
-    @pl.when(k < 2)
-    def _():
-        bring()
 
     @pl.when(k >= 2)
     def _():

time: 63.4 us -> 63.4 us (level)
  the two profiles are of different devices: /device:TPU:240 before, /device:TPU:192 now
where the time goes in v7:
time: 63.4 us; the launch traced here: 63.3 us
  Pallas kernels  62.6 us (99%)
  local copies, waits for them, and re-layouts  0.66 us (1%)
    pallas_call x1, Pallas kernels, on_device(): pl.pallas_call(functools.partial(kernel, dims), out_shape=jax.ShapeDtypeS...  62.6 us

profile of v7, /device:TPU:192, one launch (start us, length us, event | category | flops | bytes accessed | tf_op | source)
XLA Modules:
  0.0 63.3 jit_solution(3439143671504249434)
XLA Ops:
  0.0 62.6 %shard_map.55 = f32[256,128]{1,0:T(8,128)S(1)} custom-call(s32[8]{0:T(128)} %order_hbm.1, s32[8]{0:T(128)} %bitcast.1, f32[256,128]{1,0:T(8,128)} %eig_hbm.1, f32[8,1,16,512]{3,2,1,0:T(8,128)} %refl_hbm.1, f32[8,1,16,256]{3,2,1,0:T(8,128)} %fact_hbm.1), custom_call_target="tpu_custom_call" | custom-call | tf_op jit(solution)/shard_map/pallas_call | solution.py:702
  62.6 0.7 %copy.7 = f32[256,128]{1,0:T(8,128)} copy(f32[256,128]{1,0:T(8,128)S(1)} %shard_map.55) | data formatting | bytes 262144
